TPU v7x, 32 devices: a whole 2x2x4 slice. The times are simulated.
32 devices in a mesh: expert: 8 (over y, x, core), dp: 4 (over z).
Axes of the slice: x: 2, y: 2, z: 4, core: 2. Of those that a mesh axis runs over, the one named last changes fastest.
Arguments:
- tokens: bfloat16 [512, 2048], P(('expert', 'dp')), may hold values from -6 to 6
- out_grad: bfloat16 [512, 2048], P(('expert', 'dp')), may hold values from -6 to 6
- routes: int32 [512, 8], P(('expert', 'dp')), may hold values from 0 to 15, all different within a row; in each aligned block of 16 rows (0 to 15, 16 to 31, ...) at most 16 rows name the same one
- route_gates: float32 [512, 8], P(('expert', 'dp')), may hold values from 0.05 to 0.5
- w_gate: bfloat16 [16, 2048, 384], P('expert'), may hold values from -0.125 to 0.125
- w_up: bfloat16 [16, 2048, 384], P('expert'), may hold values from -0.125 to 0.125
- w_down: bfloat16 [16, 384, 2048], P('expert'), may hold values from -0.3125 to 0.3125
Outputs:
- token_grad: bfloat16 [512, 2048], P(('expert', 'dp'))
- down_grad: float32 [384, 16, 2048], P('dp', 'expert')
Inputs may be any that keep to these rules, and one draw needn't show every extreme that they name: `routes`: each row names 8 different experts. Among the 16 tokens of one device no expert is named more than 16 times, a bound that some block reaches.
All inputs are finite; a program needn't handle non-finite values.
Results may differ from a plain program's by a relative error of at most 0.014.
Values may be sent and summed in bfloat16 or wider, within the bound.
A program may use at most 64 MiB of HBM per device.

v0:
```python
import jax
import jax.numpy as jnp
from jax import lax
from jax.sharding import PartitionSpec as P


def gate_up(arrived, w_gate, w_up):
    gate_pre = jnp.einsum("erd,edf->erf", arrived, w_gate, preferred_element_type=jnp.float32)
    up_pre = jnp.einsum("erd,edf->erf", arrived, w_up, preferred_element_type=jnp.float32)
    return (gate_pre, up_pre)


def shards(tokens, out_grad, routes, route_gates, w_gate, w_up, w_down):
    tok_count, model_width = tokens.shape
    top_count = routes.shape[1]
    local_experts = w_gate.shape[0]
    groups = lax.axis_size("expert")
    experts = local_experts * groups
    slot_count = 2 * tok_count * top_count // experts
    flat_routes = routes.reshape(-1)
    onehot = (flat_routes[:, None] == jnp.arange(experts, dtype=jnp.int32)[None, :]).astype(
        jnp.int32
    )
    slot_rank = jnp.sum(onehot * (jnp.cumsum(onehot, axis=0) - onehot), axis=1)
    slot_index = flat_routes * slot_count + slot_rank
    placement = slot_index[None, :] == jnp.arange(experts * slot_count, dtype=jnp.int32)[:, None]
    route_place = placement.astype(jnp.bfloat16)
    token_place = jnp.sum(
        placement.reshape(experts * slot_count, tok_count, top_count).astype(jnp.float32), axis=2
    ).astype(jnp.bfloat16)
    send_inputs = (
        jnp.dot(token_place, tokens, preferred_element_type=jnp.float32)
        .astype(jnp.bfloat16)
        .reshape(experts, slot_count, model_width)
    )
    scaled = (
        (route_gates[:, :, None] * out_grad[:, None, :].astype(jnp.float32))
        .astype(jnp.bfloat16)
        .reshape(tok_count * top_count, model_width)
    )
    send_grads = (
        jnp.dot(route_place, scaled, preferred_element_type=jnp.float32)
        .astype(jnp.bfloat16)
        .reshape(experts, slot_count, model_width)
    )
    arrived, arrived_grad = (
        lax.all_to_all(send_inputs, "expert", split_axis=0, concat_axis=1, tiled=True),
        lax.all_to_all(send_grads, "expert", split_axis=0, concat_axis=1, tiled=True),
    )
    gate_pre, up_pre = gate_up(arrived, w_gate, w_up)
    sigmoid_gate = jax.nn.sigmoid(gate_pre)
    silu_gate = gate_pre * sigmoid_gate
    hidden = (silu_gate * up_pre).astype(jnp.bfloat16)
    hidden_grad = jnp.einsum(
        "erd,efd->erf", arrived_grad, w_down, preferred_element_type=jnp.float32
    )
    gate_grad = (
        hidden_grad * up_pre * (sigmoid_gate + gate_pre * sigmoid_gate * (1.0 - sigmoid_gate))
    ).astype(jnp.bfloat16)
    up_grad = (hidden_grad * silu_gate).astype(jnp.bfloat16)
    row_grads = (
        jnp.einsum("erf,edf->erd", gate_grad, w_gate, preferred_element_type=jnp.float32)
        + jnp.einsum("erf,edf->erd", up_grad, w_up, preferred_element_type=jnp.float32)
    ).astype(jnp.bfloat16)
    returned = lax.all_to_all(row_grads, "expert", split_axis=1, concat_axis=0, tiled=True)
    token_grad = lax.dot_general(
        token_place,
        returned.reshape(experts * slot_count, model_width),
        (((0,), (0,)), ((), ())),
        preferred_element_type=jnp.float32,
    ).astype(jnp.bfloat16)
    hidden_units = hidden.shape[2]
    share_rows = hidden_units // lax.axis_size("dp")
    partial_grad = jnp.einsum(
        "erf,erd->fed", hidden, arrived_grad, preferred_element_type=jnp.float32
    ).astype(jnp.bfloat16)
    total_grad = lax.psum(partial_grad, "dp").astype(jnp.float32)
    first_row = lax.axis_index("dp") * share_rows
    down_grad = lax.dynamic_slice_in_dim(total_grad, first_row, share_rows, 0)
    return (token_grad, down_grad)


def solution(mesh):
    placed = (
        P(("expert", "dp"), None),
        P(("expert", "dp"), None),
        P(("expert", "dp"), None),
        P(("expert", "dp"), None),
        P("expert", None, None),
        P("expert", None, None),
        P("expert", None, None),
    )
    return jax.shard_map(
        shards,
        mesh=mesh,
        in_specs=placed,
        out_specs=(P(("expert", "dp"), None), P("dp", "expert", None)),
        check_vma=False,
    )
```

profile of v0, /device:TPU:0, one launch (start us, length us, event | category | flops | bytes accessed | tf_op | source)
XLA Modules:
  0.0 193.7 jit_solution(11863418635343941623)
XLA Ops:
  7.2 0.9 copy.42
  8.2 0.1 fusion.10
  8.3 0.2 reduce_window_sum.11
  8.5 0.2 select_reduce_fusion
  8.7 0.9 convert_element_type.51
  9.5 0.8 copy.44
  10.4 1.5 convolution_convert_fusion.1
  11.8 5.2 %all-to-all-start = ((bf16[16,16,2048]{2,1,0:T(8,128)(2,1)}), bf16[16,16,2048]{2,1,0:T(8,128)(2,1)}, u32[]{:S(2)}, u32[]{:S(2)}) async-start(bf16[16,16,2048]{2,1,0:T(8,128)(2,1)} %bitcast.38), calls=%async_computation | async-start | bytes 2097152 | tf_op jit(solution)/shard_map/all_to_all | solution.py:48
  17.1 0.1 convert_reduce_fusion
  17.3 1.5 convolution_convert_fusion.2
  18.7 13.8 %all-to-all-done = bf16[16,16,2048]{2,1,0:T(8,128)(2,1)} async-done(((bf16[16,16,2048]{2,1,0:T(8,128)(2,1)}), bf16[16,16,2048]{2,1,0:T(8,128)(2,1)}, u32[]{:S(2)}, u32[]{:S(2)}) %all-to-all-start) | async-done | bytes 1048608 | tf_op jit(solution)/shard_map/all_to_all | solution.py:48
  32.5 4.2 %all-to-all-start.1 = ((bf16[16,16,2048]{2,1,0:T(8,128)(2,1)}), bf16[16,16,2048]{2,1,0:T(8,128)(2,1)}, u32[]{:S(2)}, u32[]{:S(2)}) async-start(bf16[16,16,2048]{2,1,0:T(8,128)(2,1)} %bitcast.39), calls=%async_computation.1 | async-start | bytes 2097152 | tf_op jit(solution)/shard_map/all_to_all | solution.py:47
  36.8 2.3 %copy.45 = bf16[8,2,16,2048]{3,2,0,1:T(8,128)(2,1)} copy(bf16[8,2,16,2048]{3,2,1,0:T(8,128)(2,1)} %bitcast.2) | data formatting | bytes 2097152 | tf_op jit(solution)/shard_map/all_to_all | solution.py:48
  39.1 13.0 %all-to-all-done.1 = bf16[16,16,2048]{2,1,0:T(8,128)(2,1)} async-done(((bf16[16,16,2048]{2,1,0:T(8,128)(2,1)}), bf16[16,16,2048]{2,1,0:T(8,128)(2,1)}, u32[]{:S(2)}, u32[]{:S(2)}) %all-to-all-start.1) | async-done | bytes 1048608 | tf_op jit(solution)/shard_map/all_to_all | solution.py:47
  52.2 1.5 copy.46
  53.7 0.8 fusion.19
  54.4 0.7 fusion.18
  55.2 0.8 copy-done.4
  55.9 2.7 %fusion = bf16[384,2,2048]{0,2,1:T(8,128)(2,1)} fusion(bf16[2,128,2048]{2,1,0:T(8,128)(2,1)S(1)} %bitcast.35, f32[2,128,384]{2,1,0:T(8,128)S(1)} %fusion.18, f32[2,128,384]{2,1,0:T(8,128)S(1)} %fusion.19), kind=kOutput, calls=%fused_computation.1 | convolution fusion | flops 404815872 | bytes 4980736 | tf_op jit(solution)/shard_map/erf,erd->fed/dot_general | solution.py:74
  58.7 3.3 %fusion.17 = f32[2,128,384]{2,1,0:T(8,128)S(1)} fusion(bf16[2,128,2048]{2,1,0:T(8,128)(2,1)} %bitcast.34, bf16[2,384,2048]{2,1,0:T(8,128)(2,1)} %param.13), kind=kOutput, calls=%fused_computation.31 | convolution fusion | flops 402653184 | bytes 4587520 | tf_op jit(solution)/shard_map/erd,efd->erf/dot_general | solution.py:54
  62.0 1.1 fusion.7
  63.1 0.8 copy-done.2
  63.9 1.1 fusion.1
  65.0 2.0 %copy.47 = bf16[2,128,2048]{2,0,1:T(2,128)(2,1)} copy(bf16[2,128,2048]{2,1,0:T(8,128)(2,1)S(1)} %fusion.1) | data formatting | bytes 2097152 | tf_op jit(solution)/shard_map/convert_element_type | solution.py:64
  67.1 4.2 %all-to-all-start.2 = ((bf16[2,128,2048]{2,0,1:T(2,128)(2,1)}), bf16[2,128,2048]{2,0,1:T(2,128)(2,1)}, u32[]{:S(2)}, u32[]{:S(2)}) async-start(bf16[2,128,2048]{2,0,1:T(2,128)(2,1)} %copy.47), calls=%async_computation.2 | async-start | bytes 2097152 | tf_op jit(solution)/shard_map/all_to_all | solution.py:65
  71.3 15.4 %all-to-all-done.2 = bf16[2,128,2048]{2,0,1:T(2,128)(2,1)} async-done(((bf16[2,128,2048]{2,0,1:T(2,128)(2,1)}), bf16[2,128,2048]{2,0,1:T(2,128)(2,1)}, u32[]{:S(2)}, u32[]{:S(2)}) %all-to-all-start.2) | async-done | bytes 1048608 | tf_op jit(solution)/shard_map/all_to_all | solution.py:65
  86.7 1.6 copy.48
  88.3 0.1 copy.49
  88.4 0.9 convolution_convert_fusion.3
  89.3 90.4 %all-reduce.2.cloned.1.call-done = bf16[384,2,2048]{0,2,1:T(8,128)(2,1)} async-done(((bf16[384,2,2048]{0,2,1:T(8,128)(2,1)}), bf16[384,2,2048]{0,2,1:T(8,128)(2,1)}) %all-reduce.2.cloned.1.call-update) | async-done | bytes 3145744 | tf_op jit(solution)/shard_map/psum | solution.py:77
  179.7 3.3 %dynamic-slice_convert_fusion = f32[96,2,2048]{0,2,1:T(8,128)} fusion(bf16[384,2,2048]{0,2,1:T(8,128)(2,1)} %all-reduce.2.cloned.1.call-done, s32[]{:T(128)S(6)} %select_n.3), kind=kLoop, calls=%fused_computation.7 | loop fusion | flops 393216 | bytes 2359300 | tf_op jit(solution)/shard_map/convert_element_type | solution.py:77
  183.0 3.9 %copy.51 = f32[96,2,2048]{2,1,0:T(2,128)} copy(f32[96,2,2048]{0,2,1:T(8,128)} %dynamic-slice_convert_fusion) | data formatting | bytes 3145728
  (19 shorter events, 0.4 us)
Async XLA Ops:
  7.2 46.5 %copy-start = (bf16[2,2048,384]{2,1,0:T(8,128)(2,1)S(1)}, bf16[2,2048,384]{2,1,0:T(8,128)(2,1)}, u32[]{:S(2)}) copy-start(bf16[2,2048,384]{2,1,0:T(8,128)(2,1)} %param.11) | copy-start | bytes 9437188
  7.2 10.1 %copy-start.6 = (bf16[16,2048]{1,0:T(8,128)(2,1)S(1)}, bf16[16,2048]{1,0:T(8,128)(2,1)}, u32[]{:S(2)}) copy-start(bf16[16,2048]{1,0:T(8,128)(2,1)} %param.7) | copy-start | bytes 196612
  11.8 20.7 %all-to-all-start = ((bf16[16,16,2048]{2,1,0:T(8,128)(2,1)}), bf16[16,16,2048]{2,1,0:T(8,128)(2,1)}, u32[]{:S(2)}, u32[]{:S(2)}) async-start(bf16[16,16,2048]{2,1,0:T(8,128)(2,1)} %bitcast.38), calls=%async_computation | async-start | bytes 2097152 | tf_op jit(solution)/shard_map/all_to_all | solution.py:48
  32.5 19.6 %all-to-all-start.1 = ((bf16[16,16,2048]{2,1,0:T(8,128)(2,1)}), bf16[16,16,2048]{2,1,0:T(8,128)(2,1)}, u32[]{:S(2)}, u32[]{:S(2)}) async-start(bf16[16,16,2048]{2,1,0:T(8,128)(2,1)} %bitcast.39), calls=%async_computation.1 | async-start | bytes 2097152 | tf_op jit(solution)/shard_map/all_to_all | solution.py:47
  36.8 142.9 %all-reduce.2.cloned.1.call-start = ((), (), s32[]{:S(2)}) async-start(), calls=%async_computation.3 | async-start | bytes 6291456 | tf_op jit(solution)/shard_map/psum | solution.py:77
  52.2 2.3 %copy-start.1 = (bf16[2,2048,384]{2,1,0:T(8,128)(2,1)S(1)}, bf16[2,2048,384]{2,1,0:T(8,128)(2,1)}, u32[]{:S(2)}) copy-start(bf16[2,2048,384]{2,1,0:T(8,128)(2,1)} %param.12) | copy-start | bytes 9437188
  54.4 1.5 copy-start.3
  55.1 0.8 copy-start.4
  58.6 3.3 %copy-start.5 = (f32[2,128,384]{2,1,0:T(8,128)S(1)}, f32[2,128,384]{2,1,0:T(8,128)}, u32[]{:S(2)}) copy-start(f32[2,128,384]{2,1,0:T(8,128)} %copy-done.4) | copy-start | bytes 1179652
  62.0 1.9 copy-start.2
  67.1 19.6 %all-to-all-start.2 = ((bf16[2,128,2048]{2,0,1:T(2,128)(2,1)}), bf16[2,128,2048]{2,0,1:T(2,128)(2,1)}, u32[]{:S(2)}, u32[]{:S(2)}) async-start(bf16[2,128,2048]{2,0,1:T(2,128)(2,1)} %copy.47), calls=%async_computation.2 | async-start | bytes 2097152 | tf_op jit(solution)/shard_map/all_to_all | solution.py:65
Sparse Core Ops, SparseCore 0:
  58.8 120.8 all-reduce.1
where the time goes:
time: 194 us
  waiting for transfers between devices  133 us (69%)
  local copies, waits for them, and re-layouts  14.9 us (8%)
  between operations  14.2 us (7%)
  starting transfers between devices  13.7 us (7%)
  matrix products  13.5 us (7%)
  other arithmetic  4.72 us (2%)
    psum x1, waiting for transfers between devices, shards(): total_grad = lax.psum(partial_grad, 'dp').astype(jnp.float32)  90.4 us
    all_to_all x1, waiting for transfers between devices, shards(): lax.all_to_all(row_grads, 'expert', split_axis=1, concat_axis=0, tiled=True)  15.4 us
    all_to_all x1, waiting for transfers between devices, shards(): lax.all_to_all(send_grads, 'expert', split_axis=0, concat_axis=1, tiled=T...  13.8 us
    all_to_all x1, waiting for transfers between devices, shards(): lax.all_to_all(send_inputs, 'expert', split_axis=0, concat_axis=1, tiled=...  13 us
    unnamed x17, local copies, waits for them, and re-layouts  7.11 us
    all_to_all x1, starting transfers between devices, shards(): lax.all_to_all(send_grads, 'expert', split_axis=0, concat_axis=1, tiled=T...  5.2 us
    all_to_all x1, starting transfers between devices, shards(): lax.all_to_all(row_grads, 'expert', split_axis=1, concat_axis=0, tiled=True)  4.25 us
    all_to_all x1, starting transfers between devices, shards(): lax.all_to_all(send_inputs, 'expert', split_axis=0, concat_axis=1, tiled=...  4.24 us
  transfers between devices with their start and end apart: 4, of which 4 were waited for; matrix products, arithmetic and copies ran while one was open for 7% of the time, Pallas kernels for 0%

commit v1 on v0

--- a/solution.py
+++ b/solution.py
@@ -45,7 +45,12 @@
     )
     arrived, arrived_grad = (
         lax.all_to_all(send_inputs, "expert", split_axis=0, concat_axis=1, tiled=True),
-        lax.all_to_all(send_grads, "expert", split_axis=0, concat_axis=1, tiled=True),
+        jnp.concatenate(
+            lax.all_to_all(
+                jnp.stack(jnp.split(send_grads, lax.axis_size("expert"), axis=0)), "expert", 0, 0
+            ),
+            axis=1,
+        ),
     )
     gate_pre, up_pre = gate_up(arrived, w_gate, w_up)
     sigmoid_gate = jax.nn.sigmoid(gate_pre)

time: 194 us -> 200 us (1.031)
  local copies, waits for them, and re-layouts: 14.9 us -> 19.8 us
    unnamed x17 -> x22, local copies, waits for them, and re-layouts: 7.11 us -> 11.4 us
    all_to_all x1 -> x0, local copies, waits for them, and re-layouts: 2.3 us -> none  [shards(): lax.all_to_all(send_grads, 'expert', split_axis=0, concat_axis=1, tiled=T...]
    reshape x0 -> x1, local copies, waits for them, and re-layouts: none -> 2.3 us  [shards(): jnp.concatenate(lax.all_to_all(jnp.stack(jnp.split(send_grads, lax.axis_s...]
where the time goes in v1:
time: 200 us
  waiting for transfers between devices  133 us (66%)
  local copies, waits for them, and re-layouts  19.8 us (10%)
  matrix products  14.5 us (7%)
  between operations  14.2 us (7%)
  starting transfers between devices  13.7 us (7%)
  other arithmetic  4.87 us (2%)
    psum x1, waiting for transfers between devices, shards(): total_grad = lax.psum(partial_grad, 'dp').astype(jnp.float32)  90.4 us
    all_to_all x1, waiting for transfers between devices, shards(): lax.all_to_all(row_grads, 'expert', split_axis=1, concat_axis=0, tiled=True)  15.4 us
    all_to_all x1, waiting for transfers between devices, shards(): lax.all_to_all(jnp.stack(jnp.split(send_grads, lax.axis_size('expert'), a...  13.8 us
    all_to_all x1, waiting for transfers between devices, shards(): lax.all_to_all(send_inputs, 'expert', split_axis=0, concat_axis=1, tiled=...  13 us
    unnamed x22, local copies, waits for them, and re-layouts  11.4 us
    all_to_all x1, starting transfers between devices, shards(): lax.all_to_all(jnp.stack(jnp.split(send_grads, lax.axis_size('expert'), a...  5.2 us
    all_to_all x1, starting transfers between devices, shards(): lax.all_to_all(row_grads, 'expert', split_axis=1, concat_axis=0, tiled=True)  4.25 us
    all_to_all x1, starting transfers between devices, shards(): lax.all_to_all(send_inputs, 'expert', split_axis=0, concat_axis=1, tiled=...  4.24 us
  transfers between devices with their start and end apart: 4, of which 4 were waited for; matrix products, arithmetic and copies ran while one was open for 7% of the time, Pallas kernels for 0%

profile of v1, /device:TPU:0, one launch (start us, length us, event | category | flops | bytes accessed | tf_op | source)
XLA Modules:
  0.0 199.7 jit_solution(2761367464395718994)
XLA Ops:
  7.2 1.0 convert_element_type.51
  8.2 0.8 copy.44
  9.0 0.8 copy.42
  10.9 0.7 constant_dynamic-update-slice_fusion.7
  11.6 0.7 constant_dynamic-update-slice_fusion.6
  12.3 0.7 constant_dynamic-update-slice_fusion.5
  12.9 0.7 constant_dynamic-update-slice_fusion.4
  13.6 0.7 constant_dynamic-update-slice_fusion.3
  14.3 0.7 constant_dynamic-update-slice_fusion.2
  14.9 0.7 constant_dynamic-update-slice_fusion.1
  16.2 5.2 %all-to-all-start = ((bf16[8,2,16,2048]{3,2,1,0:T(8,128)(2,1)}), bf16[8,2,16,2048]{3,2,1,0:T(8,128)(2,1)}, u32[]{:S(2)}, u32[]{:S(2)}) async-start(bf16[8,2,16,2048]{3,2,1,0:T(8,128)(2,1)} %constant_dynamic-update-slice_fusion), calls=%async_computation | async-start | bytes 2097152 | tf_op jit(solution)/shard_map/all_to_all | solution.py:49
  21.7 1.5 convolution_convert_fusion.2
  23.1 13.8 %all-to-all-done = bf16[8,2,16,2048]{3,2,1,0:T(8,128)(2,1)} async-done(((bf16[8,2,16,2048]{3,2,1,0:T(8,128)(2,1)}), bf16[8,2,16,2048]{3,2,1,0:T(8,128)(2,1)}, u32[]{:S(2)}, u32[]{:S(2)}) %all-to-all-start) | async-done | bytes 1048608 | tf_op jit(solution)/shard_map/all_to_all | solution.py:49
  36.9 4.2 %all-to-all-start.1 = ((bf16[16,16,2048]{2,1,0:T(8,128)(2,1)}), bf16[16,16,2048]{2,1,0:T(8,128)(2,1)}, u32[]{:S(2)}, u32[]{:S(2)}) async-start(bf16[16,16,2048]{2,1,0:T(8,128)(2,1)} %bitcast.43), calls=%async_computation.1 | async-start | bytes 2097152 | tf_op jit(solution)/shard_map/all_to_all | solution.py:47
  41.2 2.3 %copy.45 = bf16[2,8,16,2048]{3,2,1,0:T(8,128)(2,1)} copy(bf16[2,8,16,2048]{3,2,0,1:T(8,128)(2,1)} %bitcast.9) | data formatting | bytes 2097152 | tf_op jit(solution)/shard_map/reshape | solution.py:48
  43.5 13.0 %all-to-all-done.1 = bf16[16,16,2048]{2,1,0:T(8,128)(2,1)} async-done(((bf16[16,16,2048]{2,1,0:T(8,128)(2,1)}), bf16[16,16,2048]{2,1,0:T(8,128)(2,1)}, u32[]{:S(2)}, u32[]{:S(2)}) %all-to-all-start.1) | async-done | bytes 1048608 | tf_op jit(solution)/shard_map/all_to_all | solution.py:47
  56.6 1.3 copy.46
  57.9 2.7 %fusion.19 = f32[2,128,384]{2,1,0:T(8,128)S(1)} fusion(bf16[2,128,2048]{2,1,0:T(8,128)(2,1)S(1)} %bitcast.41, bf16[2,2048,384]{2,1,0:T(8,128)(2,1)} %param.12), kind=kOutput, calls=%fused_computation.41 | convolution fusion | flops 402653184 | bytes 4587520 | tf_op jit(solution)/shard_map/erd,edf->erf/dot_general | solution.py:9
  60.6 0.8 fusion.20
  61.9 2.7 %fusion = bf16[384,2,2048]{0,2,1:T(8,128)(2,1)} fusion(bf16[2,128,2048]{2,1,0:T(8,128)(2,1)S(1)} %bitcast.40, f32[2,128,384]{2,1,0:T(8,128)S(1)} %fusion.19, f32[2,128,384]{2,1,0:T(8,128)S(1)} %fusion.20), kind=kOutput, calls=%fused_computation.1 | convolution fusion | flops 404815872 | bytes 4980736 | tf_op jit(solution)/shard_map/erf,erd->fed/dot_general | solution.py:79
  64.7 3.3 %fusion.18 = f32[2,128,384]{2,1,0:T(8,128)S(1)} fusion(bf16[2,128,2048]{2,1,0:T(8,128)(2,1)} %bitcast.39, bf16[2,384,2048]{2,1,0:T(8,128)(2,1)} %param.13), kind=kOutput, calls=%fused_computation.40 | convolution fusion | flops 402653184 | bytes 4587520 | tf_op jit(solution)/shard_map/erd,efd->erf/dot_general | solution.py:59
  68.0 1.1 fusion.7
  69.2 0.8 copy-done.1
  69.9 1.1 fusion.1
  71.0 2.0 %copy.47 = bf16[2,128,2048]{2,0,1:T(2,128)(2,1)} copy(bf16[2,128,2048]{2,1,0:T(8,128)(2,1)S(1)} %fusion.1) | data formatting | bytes 2097152 | tf_op jit(solution)/shard_map/convert_element_type | solution.py:69
  73.1 4.2 %all-to-all-start.2 = ((bf16[2,128,2048]{2,0,1:T(2,128)(2,1)}), bf16[2,128,2048]{2,0,1:T(2,128)(2,1)}, u32[]{:S(2)}, u32[]{:S(2)}) async-start(bf16[2,128,2048]{2,0,1:T(2,128)(2,1)} %copy.47), calls=%async_computation.2 | async-start | bytes 2097152 | tf_op jit(solution)/shard_map/all_to_all | solution.py:70
  77.4 15.4 %all-to-all-done.2 = bf16[2,128,2048]{2,0,1:T(2,128)(2,1)} async-done(((bf16[2,128,2048]{2,0,1:T(2,128)(2,1)}), bf16[2,128,2048]{2,0,1:T(2,128)(2,1)}, u32[]{:S(2)}, u32[]{:S(2)}) %all-to-all-start.2) | async-done | bytes 1048608 | tf_op jit(solution)/shard_map/all_to_all | solution.py:70
  92.7 1.6 copy.48
  94.4 0.9 convolution_convert_fusion.3
  95.3 90.4 %all-reduce.2.cloned.1.call-done = bf16[384,2,2048]{0,2,1:T(8,128)(2,1)} async-done(((bf16[384,2,2048]{0,2,1:T(8,128)(2,1)}), bf16[384,2,2048]{0,2,1:T(8,128)(2,1)}) %all-reduce.2.cloned.1.call-update) | async-done | bytes 3145744 | tf_op jit(solution)/shard_map/psum | solution.py:82
  185.7 3.3 %dynamic-slice_convert_fusion = f32[96,2,2048]{0,2,1:T(8,128)} fusion(bf16[384,2,2048]{0,2,1:T(8,128)(2,1)} %all-reduce.2.cloned.1.call-done, s32[]{:T(128)S(6)} %select_n.3), kind=kLoop, calls=%fused_computation.7 | loop fusion | flops 393216 | bytes 2359300 | tf_op jit(solution)/shard_map/convert_element_type | solution.py:82
  189.0 3.9 %copy.51 = f32[96,2,2048]{2,1,0:T(2,128)} copy(f32[96,2,2048]{0,2,1:T(8,128)} %dynamic-slice_convert_fusion) | data formatting | bytes 3145728
  (26 shorter events, 2.8 us)
Async XLA Ops:
  7.2 53.4 %copy-start = (bf16[2,2048,384]{2,1,0:T(8,128)(2,1)S(1)}, bf16[2,2048,384]{2,1,0:T(8,128)(2,1)}, u32[]{:S(2)}) copy-start(bf16[2,2048,384]{2,1,0:T(8,128)(2,1)} %param.11) | copy-start | bytes 9437188
  10.8 10.8 %copy-start.5 = (bf16[16,2048]{1,0:T(8,128)(2,1)S(1)}, bf16[16,2048]{1,0:T(8,128)(2,1)}, u32[]{:S(2)}) copy-start(bf16[16,2048]{1,0:T(8,128)(2,1)} %param.7) | copy-start | bytes 196612
  16.2 20.7 %all-to-all-start = ((bf16[8,2,16,2048]{3,2,1,0:T(8,128)(2,1)}), bf16[8,2,16,2048]{3,2,1,0:T(8,128)(2,1)}, u32[]{:S(2)}, u32[]{:S(2)}) async-start(bf16[8,2,16,2048]{3,2,1,0:T(8,128)(2,1)} %constant_dynamic-update-slice_fusion), calls=%async_computation | async-start | bytes 2097152 | tf_op jit(solution)/shard_map/all_to_all | solution.py:49
  36.9 19.6 %all-to-all-start.1 = ((bf16[16,16,2048]{2,1,0:T(8,128)(2,1)}), bf16[16,16,2048]{2,1,0:T(8,128)(2,1)}, u32[]{:S(2)}, u32[]{:S(2)}) async-start(bf16[16,16,2048]{2,1,0:T(8,128)(2,1)} %bitcast.43), calls=%async_computation.1 | async-start | bytes 2097152 | tf_op jit(solution)/shard_map/all_to_all | solution.py:47
  41.2 144.5 %all-reduce.2.cloned.1.call-start = ((), (), s32[]{:S(2)}) async-start(), calls=%async_computation.3 | async-start | bytes 6291456 | tf_op jit(solution)/shard_map/psum | solution.py:82
  60.6 0.8 copy-start.3
  60.6 1.4 copy-start.2
  64.7 3.3 %copy-start.4 = (f32[2,128,384]{2,1,0:T(8,128)S(1)}, f32[2,128,384]{2,1,0:T(8,128)}, u32[]{:S(2)}) copy-start(f32[2,128,384]{2,1,0:T(8,128)} %copy-done.3) | copy-start | bytes 1179652
  68.0 1.9 copy-start.1
  73.1 19.6 %all-to-all-start.2 = ((bf16[2,128,2048]{2,0,1:T(2,128)(2,1)}), bf16[2,128,2048]{2,0,1:T(2,128)(2,1)}, u32[]{:S(2)}, u32[]{:S(2)}) async-start(bf16[2,128,2048]{2,0,1:T(2,128)(2,1)} %copy.47), calls=%async_computation.2 | async-start | bytes 2097152 | tf_op jit(solution)/shard_map/all_to_all | solution.py:70
Sparse Core Ops, SparseCore 0:
  64.8 120.8 all-reduce.1
